TPU v7x, 512 devices: a whole 4x4x16 slice. The times are simulated.
512 devices in a mesh: inst: 16 (over y_lo, x, core), sector: 32 (over y_hi, z).
Axes of the slice: x: 4, y: 4 (y_hi: 2, y_lo: 2; y = y_hi * 2 + y_lo), z: 16, core: 2. Of those that a mesh axis runs over, the one named last changes fastest.
Arguments:
- lam_init: float32 [16, 512, 32, 128], P('inst', 'sector'), may hold values from -6 to 6
- rhs: float32 [16, 512, 32, 128], P('inst', 'sector'), may hold values from -6 to 6
- relax: float32 [16, 512, 128], P('inst', 'sector'), may hold values from 0.15 to 0.6
- cond: float32 [512, 128], P('sector'), may hold values from 0.05 to 0.4
- jac: bfloat16 [16, 512, 6, 128, 128], P('inst', 'sector'), may hold values from -0.21875 to 0.21875
- rotor_jac: bfloat16 [16, 128, 128, 128], P('inst', 'sector'), may hold values from -0.5 to 0.5
- cols: int32 [512, 6], P('sector'), may hold values from 0 to 17
- rotor_shift: int32 [16, 128], P('inst', 'sector'), may hold values from 0 to 1
- owned: int32 [32], P('sector'), may hold values from 1 to 12, 288 in all
Outputs:
- adjoint: float32 [16, 512, 32, 128], P('inst', 'sector')
All inputs are finite; a program needn't handle non-finite values. No bound on the sum of `owned` on one device may be relied on, other than what follows from the above.
Results may differ from a plain program's by a relative error of at most 0.002.
Values may be sent and summed in bfloat16 or wider, within the bound.
No kernel may reach another device: no remote copies, remote signals or barrier semaphores. Data moves between devices by JAX's collectives and lax.ppermute only.
A program may use at most 64 MiB of HBM per device.

v0:
```python
import jax
import jax.numpy as jnp
from jax import lax
from jax.sharding import PartitionSpec as P

NT = 16
SWEEPS = 2


def padded(cells, sides, width):
    for axis, dim in sides:
        count = lax.axis_size(axis)
        head = lax.slice_in_dim(cells, 0, width, axis=dim)
        tail = lax.slice_in_dim(cells, cells.shape[dim] - width, cells.shape[dim], axis=dim)
        cells = jnp.concatenate(
            [
                lax.ppermute(tail, axis, [(i, (i + 1) % count) for i in range(count)]),
                cells,
                lax.ppermute(head, axis, [((i + 1) % count, i) for i in range(count)]),
            ],
            axis=dim,
        )
    return cells


def shifted(block, axis, distance):
    devices = range(lax.axis_size(axis))
    route = [((i - distance) % len(devices), i) for i in devices]
    return lax.ppermute(block, axis, route)


def spectral_matrix():
    index = jnp.arange(NT)
    offset = index[:, None] - index[None, :]
    angle = jnp.pi * offset.astype(jnp.float32) / NT
    safe_sin = jnp.where(offset == 0, jnp.float32(1.0), jnp.sin(angle))
    parity = jnp.where(offset % 2 == 0, jnp.float32(1.0), jnp.float32(-1.0))
    deriv = jnp.where(offset == 0, jnp.float32(0.0), 0.5 * parity * jnp.cos(angle) / safe_sin)
    return deriv + jnp.float32(2.0) / NT


def shards(lam_init, rhs, relax, cond, jac, rotor_jac, cols, rotor_shift, owned):
    local_inst = lam_init.shape[0]
    rows = lam_init.shape[1]
    rotor_rows = rotor_jac.shape[1]
    dspec = spectral_matrix()
    first_inst = lax.axis_index("inst") * local_inst
    row = jnp.arange(rows)
    live = ((row >= rows - rotor_rows) | (row < owned[0])).astype(jnp.float32)[None, :, None, None]
    lam = lam_init * live
    moving = rotor_shift.astype(jnp.float32)[:, :, None, None]
    relax_wide = relax[:, :, None, :]
    cond_wide = cond[None, :, None, :]
    for sweep in range(SWEEPS):
        lam_b = lam.astype(jnp.bfloat16)
        lam_h = padded(lam_b, (("sector", 1),), 1)
        picked = lam_h[:, cols]
        stator = jnp.einsum("tnkri,tnkio->tnro", picked, jac, preferred_element_type=jnp.float32)
        records = jnp.einsum(
            "tjri,tjio->tjro",
            lam_b[:, rows - rotor_rows :],
            rotor_jac,
            preferred_element_type=jnp.float32,
        )
        arrived = shifted((records * moving).astype(jnp.bfloat16), "sector", 1).astype(jnp.float32)
        rotor = records * (1.0 - moving) + arrived
        rotor_full = jnp.concatenate(
            [jnp.zeros((local_inst, rows - rotor_rows) + rotor.shape[2:], jnp.float32), rotor],
            axis=1,
        )
        weighted = lam * cond_wide
        piece = lax.all_gather(weighted, "inst", axis=0, tiled=True)
        coef = lax.dynamic_slice(dspec, (0, first_inst), (piece.shape[0], local_inst))
        spec = jnp.zeros_like(weighted) + jnp.einsum(
            "jt,jnrc->tnrc", coef, piece, precision=lax.Precision.HIGHEST
        )
        resid = rhs - (stator + rotor_full + spec)
        lam = lam + relax_wide * resid * live
    return lam


def solution(mesh):
    return jax.shard_map(
        shards,
        mesh=mesh,
        in_specs=(
            P("inst", "sector", None, None),
            P("inst", "sector", None, None),
            P("inst", "sector", None),
            P("sector", None),
            P("inst", "sector", None, None, None),
            P("inst", "sector", None, None),
            P("sector", None),
            P("inst", "sector"),
            P("sector"),
        ),
        out_specs=P("inst", "sector", None, None),
        check_vma=False,
    )
```

profile of v0, /device:TPU:1, one launch (start us, length us, event | category | flops | bytes accessed | tf_op | source)
XLA Modules:
  0.0 128.8 jit_solution(6784059207675336559)
XLA Ops:
  6.5 0.0 copy-start
  6.5 0.0 all-gather.3.cloned.1.call-start
  7.4 0.0 copy-start.17
  7.4 1.9 %multiply_convert_fusion = (bf16[1,16,32,128]{3,2,1,0:T(8,128)(2,1)S(1)}, f32[1,16,32,128]{3,2,1,0:T(8,128)}) fusion(f32[1,16,32,128]{3,2,1,0:T(8,128)} %param.9, f32[16]{0:T(128)S(1)} %or_convert_fusion, f32[16,128]{1,0:T(8,128)} %param.12), kind=kLoop, calls=%fused_computation.15 | loop fusion | flops 196608 | bytes 663616 | tf_op jit(solution)/shard_map/convert_element_type | solution.py:55
  9.3 0.0 all-gather.3.cloned.1.call-update
  9.3 0.0 all-gather.5.cloned.1.call-start
  9.3 0.7 convert_bitcast_fusion
  10.0 0.0 copy-done.17
  10.0 1.1 fusion.16
  11.1 0.7 fusion.18
  11.7 4.4 %collective-permute-start.2 = (bf16[1,4,32,128]{3,2,1,0:T(8,128)(2,1)}, bf16[1,4,32,128]{3,2,1,0:T(8,128)(2,1)S(1)}, u32[]{:S(2)}, u32[]{:S(2)}) collective-permute-start(bf16[1,4,32,128]{3,2,1,0:T(8,128)(2,1)} %fusion.18), channel_id=1, source_target_pairs={{31,0},{0,1},{1,2},{2,3},{3,4},{4,5},{5,6},{6,7},{7,8},{8,9},{9,10... | collective-permute-start | bytes 98312 | tf_op jit(solution)/shard_map/ppermute | solution.py:29
  16.1 0.0 copy-done.20
  16.1 12.1 %collective-permute-start.1 = (bf16[1,1,32,128]{3,2,1,0:T(8,128)(2,1)S(1)}, bf16[1,1,32,128]{3,2,1,0:T(8,128)(2,1)S(1)}, u32[]{:S(2)}, u32[]{:S(2)}) collective-permute-start(bf16[1,1,32,128]{3,2,1,0:T(8,128)(2,1)S(1)} %get-tuple-element.12), channel_id=1, source_target_pairs={{1,0},{2,1},{3,2},{4,3},{5,4},{6,5},{7,6},{8,7},{9,8},{10,9},{11,1... | collective-permute-start | bytes 24584 | tf_op jit(solution)/shard_map/ppermute | solution.py:19
  28.3 1.9 %collective-permute-start = (bf16[1,1,32,128]{3,2,1,0:T(8,128)(2,1)S(1)}, bf16[1,1,32,128]{3,2,1,0:T(8,128)(2,1)}, u32[]{:S(2)}, u32[]{:S(2)}) collective-permute-start(bf16[1,1,32,128]{3,2,1,0:T(8,128)(2,1)S(1)} %get-tuple-element.11), channel_id=1, source_target_pairs={{0,1},{1,2},{2,3},{3,4},{4,5},{5,6},{6,7},{7,8},{8,9},{9,10},{10,1... | collective-permute-start | bytes 24584 | tf_op jit(solution)/shard_map/ppermute | solution.py:17
  30.2 0.7 compare_select_fusion
  30.9 0.1 copy.12
  31.0 0.1 reshape.75
  31.1 0.0 copy-start.9
  31.1 0.0 copy-start.13
  31.1 0.0 copy-start.14
  31.1 1.2 broadcast_subtract_fusion
  32.3 0.0 collective-permute-done.1
  32.3 0.0 copy-start.15
  32.3 0.6 copy-done.15
  32.9 3.6 %collective-permute-done = bf16[1,1,32,128]{3,2,1,0:T(8,128)(2,1)} collective-permute-done((bf16[1,1,32,128]{3,2,1,0:T(8,128)(2,1)S(1)}, bf16[1,1,32,128]{3,2,1,0:T(8,128)(2,1)}, u32[]{:S(2)}, u32[]{:S(2)}) %collective-permute-start) | collective-permute-done | bytes 8224 | tf_op jit(solution)/shard_map/ppermute | solution.py:17
  36.5 0.7 maximum_bitcast_fusion
  37.2 1.6 %gather_fusion = bf16[96,32,128]{2,1,0:T(8,128)(2,1)} fusion(bf16[18,32,128]{2,1,0:T(8,128)(2,1)S(1)} %maximum_bitcast_fusion, s32[1024]{0:T(1024)S(1)} %pad_clamp_fusion), kind=kCustom, calls=%fused_computation | custom fusion | bytes 1573248 | tf_op jit(solution)/shard_map/gather | solution.py:57
  38.8 0.0 collective-permute-done.2
  38.8 1.3 %bitcast_add_fusion.1 = f32[1,4,32,128]{3,2,1,0:T(8,128)} fusion(bf16[1,4,32,128]{3,2,1,0:T(8,128)(2,1)S(1)} %collective-permute-done.2, f32[4,32,128]{2,1,0:T(8,128)S(1)} %fusion.16, f32[4]{0:T(128)} %broadcast_subtract_fusion), kind=kLoop, calls=%fused_computation.24 | loop fusion | flops 49152 | bytes 163856 | tf_op jit(solution)/shard_map/add | solution.py:66
  40.1 20.2 %all-gather.3.cloned.1.call-done = f32[16,16,32,128]{3,2,1,0:T(8,128)} async-done(((f32[1,16,32,128]{3,2,1,0:T(8,128)}), f32[16,16,32,128]{3,2,1,0:T(8,128)}) %all-gather.3.cloned.1.call-update) | async-done | bytes 4194320 | tf_op jit(solution)/shard_map/all_gather | solution.py:72
  60.4 0.0 copy-start.10
  60.4 6.5 %fusion.2 = f32[1,16,32,128]{3,0,2,1:T(1,128)S(1)} fusion(f32[16,16,32,128]{3,2,1,0:T(8,128)} %all-gather.3.cloned.1.call-done, f32[16,16]{0,1:T(8,128)S(1)} %get-tuple-element.14, s32[]{:T(128)S(6)} %select_n.31, pred[16,16]{0,1:T(8,128)(4,1)S(1)} %fusion.21, s32[16,16]{0,1:T(8,128)S(1)} %get-tuple-element.13), kind=kOutput, calls=%fused_computation.4 | convolution fusion | flops 12583056 | bytes 4457988 | tf_op jit(solution)/shard_map/jt,jnrc->tnrc/dot_general | solution.py:74
  66.9 0.0 copy-done.9
  66.9 0.0 copy-done.13
  67.0 0.0 copy-done.16
  67.0 0.0 copy-done
  67.0 0.0 copy-done.11
  67.0 0.0 copy-done.2
  67.0 0.0 copy-done.3
  67.0 0.0 copy-done.4
  67.0 0.0 copy-done.8
  67.0 0.0 copy-done.18
  67.0 0.7 fusion.32
  67.7 0.0 copy-done.14
  67.7 0.0 copy-start.6
  67.7 0.0 copy-done.10
  67.7 0.7 broadcast_multiply_fusion
  68.5 0.0 all-gather.5.cloned.1.call-update
  68.5 7.7 %collective-permute-start.4 = (bf16[1,1,32,128]{3,2,1,0:T(8,128)(2,1)S(1)}, bf16[1,1,32,128]{3,2,1,0:T(8,128)(2,1)S(1)}, u32[]{:S(2)}, u32[]{:S(2)}) collective-permute-start(bf16[1,1,32,128]{3,2,1,0:T(8,128)(2,1)S(1)} %get-tuple-element.10), channel_id=1, source_target_pairs={{1,0},{2,1},{3,2},{4,3},{5,4},{6,5},{7,6},{8,7},{9,8},{10,9},{11,1... | collective-permute-start | bytes 24584 | tf_op jit(solution)/shard_map/ppermute | solution.py:19
  76.3 1.9 %collective-permute-start.3 = (bf16[1,1,32,128]{3,2,1,0:T(8,128)(2,1)S(1)}, bf16[1,1,32,128]{3,2,1,0:T(8,128)(2,1)S(1)}, u32[]{:S(2)}, u32[]{:S(2)}) collective-permute-start(bf16[1,1,32,128]{3,2,1,0:T(8,128)(2,1)S(1)} %get-tuple-element.9), channel_id=1, source_target_pairs={{0,1},{1,2},{2,3},{3,4},{4,5},{5,6},{6,7},{7,8},{8,9},{9,10},{10,1... | collective-permute-start | bytes 24584 | tf_op jit(solution)/shard_map/ppermute | solution.py:17
  78.2 1.1 fusion.14
  79.2 1.4 %fusion.19 = bf16[1,4,32,128]{3,2,1,0:T(8,128)(2,1)} fusion(f32[4,32,128]{2,1,0:T(8,128)S(1)} %fusion.14, f32[4]{0:T(128)} %copy-done.20), kind=kLoop, calls=%fused_computation.28 | loop fusion | flops 32768 | bytes 98320 | tf_op jit(solution)/shard_map/convert_element_type | solution.py:65
  80.6 1.9 %collective-permute-start.5 = (bf16[1,4,32,128]{3,2,1,0:T(8,128)(2,1)}, bf16[1,4,32,128]{3,2,1,0:T(8,128)(2,1)}, u32[]{:S(2)}, u32[]{:S(2)}) collective-permute-start(bf16[1,4,32,128]{3,2,1,0:T(8,128)(2,1)} %fusion.19), channel_id=1, source_target_pairs={{31,0},{0,1},{1,2},{2,3},{3,4},{4,5},{5,6},{6,7},{7,8},{8,9},{9,10... | collective-permute-start | bytes 98312 | tf_op jit(solution)/shard_map/ppermute | solution.py:29
  82.5 0.0 collective-permute-done.4
  82.5 0.0 copy-done.6
  82.5 1.7 %collective-permute-done.3 = bf16[1,1,32,128]{3,2,1,0:T(8,128)(2,1)S(1)} collective-permute-done((bf16[1,1,32,128]{3,2,1,0:T(8,128)(2,1)S(1)}, bf16[1,1,32,128]{3,2,1,0:T(8,128)(2,1)S(1)}, u32[]{:S(2)}, u32[]{:S(2)}) %collective-permute-start.3) | collective-permute-done | bytes 8224 | tf_op jit(solution)/shard_map/ppermute | solution.py:17
  84.3 0.0 copy-done.7
  84.3 0.9 maximum_bitcast_fusion.1
  85.2 1.7 %gather_fusion.1 = bf16[96,32,128]{2,1,0:T(8,128)(2,1)} fusion(bf16[18,32,128]{2,1,0:T(8,128)(2,1)S(1)} %maximum_bitcast_fusion.1, s32[1024]{0:T(1024)} %copy-done.9), kind=kCustom, calls=%fused_computation.1 | custom fusion | bytes 1573248 | tf_op jit(solution)/shard_map/gather | solution.py:57
  86.9 2.4 %collective-permute-done.5 = bf16[1,4,32,128]{3,2,1,0:T(8,128)(2,1)} collective-permute-done((bf16[1,4,32,128]{3,2,1,0:T(8,128)(2,1)}, bf16[1,4,32,128]{3,2,1,0:T(8,128)(2,1)}, u32[]{:S(2)}, u32[]{:S(2)}) %collective-permute-start.5) | collective-permute-done | bytes 32800 | tf_op jit(solution)/shard_map/ppermute | solution.py:29
  89.3 0.9 bitcast_add_fusion
  90.2 23.8 %all-gather.5.cloned.1.call-done = f32[16,16,32,128]{3,2,1,0:T(8,128)} async-done(((f32[1,16,32,128]{3,2,1,0:T(8,128)}), f32[16,16,32,128]{3,2,1,0:T(8,128)}) %all-gather.5.cloned.1.call-update) | async-done | bytes 4194320 | tf_op jit(solution)/shard_map/all_gather | solution.py:72
  114.0 6.5 %fusion = f32[1,16,32,128]{3,0,2,1:T(1,128)S(1)} fusion(f32[16,16,32,128]{3,2,1,0:T(8,128)} %all-gather.5.cloned.1.call-done, f32[16,16]{0,1:T(8,128)} %copy-done.14, s32[]{:T(128)S(6)} %select_n.31, pred[16,16]{0,1:T(8,128)(4,1)} %copy-done.16, s32[16,16]{0,1:T(8,128)} %copy-done.13), kind=kOutput, calls=%fused_computation.2 | convolution fusion | flops 12583056 | bytes 4457988 | tf_op jit(solution)/shard_map/jt,jnrc->tnrc/dot_general | solution.py:74
  120.5 1.4 %multiply_add_fusion = f32[1,16,32,128]{3,2,1,0:T(8,128)} fusion(f32[1,16,32,128]{3,2,1,0:T(8,128)S(1)} %get-tuple-element.6, f32[1,16,32,128]{3,2,1,0:T(8,128)S(1)} %copy-done.5, f32[1,16,32,128]{3,2,1,0:T(8,128)S(1)} %bitcast.74, f32[1,4,32,128]{3,2,1,0:T(8,128)S(1)} %bitcast_add_fusion, f32[16,128]{1,0:T(8,128)S(1)} %bitcast.77, f32[16]{0:T(128)S(1)} %copy-done.19, ...), kind=kOutput, calls=%fused_computation.12 | convolution fusion | flops 101056512 | bytes 5054528 | tf_op jit(solution)/shard_map/tnkri,tnkio->tnro/dot_general | solution.py:58
  (23 shorter events, 0.1 us)
Async XLA Ops:
  6.5 60.4 %copy-start = (bf16[1,16,6,128,128]{4,3,2,1,0:T(8,128)(2,1)S(1)}, bf16[1,16,6,128,128]{4,3,2,1,0:T(8,128)(2,1)}, u32[]{:S(2)}) copy-start(bf16[1,16,6,128,128]{4,3,2,1,0:T(8,128)(2,1)} %param.13) | copy-start | bytes 9437188
  6.5 60.4 %copy-start.11 = (f32[1,16,128]{2,1,0:T(8,128)S(1)}, f32[1,16,128]{2,1,0:T(8,128)}, u32[]{:S(2)}) copy-start(f32[1,16,128]{2,1,0:T(8,128)} %param.11) | copy-start | bytes 24580
  6.5 53.8 %all-gather.3.cloned.1.call-start = ((), (), s32[]{:S(2)}) async-start(), calls=%async_computation | async-start | bytes 4456448 | tf_op jit(solution)/shard_map/all_gather | solution.py:72
  7.4 2.7 %copy-start.17 = (f32[16]{0:T(128)}, f32[16]{0:T(128)S(1)}, u32[]{:S(2)}) copy-start(f32[16]{0:T(128)S(1)} %or_convert_fusion) | copy-start | bytes 196
  9.3 104.7 %all-gather.5.cloned.1.call-start = ((), (), s32[]{:S(2)}) async-start(), calls=%async_computation.1 | async-start | bytes 4456448 | tf_op jit(solution)/shard_map/all_gather | solution.py:72
  10.0 6.1 %copy-start.20 = (f32[4]{0:T(128)}, f32[4]{0:T(128)S(1)}, u32[]{:S(2)}) copy-start(f32[4]{0:T(128)S(1)} %convert_bitcast_fusion) | copy-start | bytes 52
  11.7 27.1 %collective-permute-start.2 = (bf16[1,4,32,128]{3,2,1,0:T(8,128)(2,1)}, bf16[1,4,32,128]{3,2,1,0:T(8,128)(2,1)S(1)}, u32[]{:S(2)}, u32[]{:S(2)}) collective-permute-start(bf16[1,4,32,128]{3,2,1,0:T(8,128)(2,1)} %fusion.18), channel_id=1, source_target_pairs={{31,0},{0,1},{1,2},{2,3},{3,4},{4,5},{5,6},{6,7},{7,8},{8,9},{9,10... | collective-permute-start | bytes 98312 | tf_op jit(solution)/shard_map/ppermute | solution.py:29
  16.1 16.2 %collective-permute-start.1 = (bf16[1,1,32,128]{3,2,1,0:T(8,128)(2,1)S(1)}, bf16[1,1,32,128]{3,2,1,0:T(8,128)(2,1)S(1)}, u32[]{:S(2)}, u32[]{:S(2)}) collective-permute-start(bf16[1,1,32,128]{3,2,1,0:T(8,128)(2,1)S(1)} %get-tuple-element.12), channel_id=1, source_target_pairs={{1,0},{2,1},{3,2},{4,3},{5,4},{6,5},{7,6},{8,7},{9,8},{10,9},{11,1... | collective-permute-start | bytes 24584 | tf_op jit(solution)/shard_map/ppermute | solution.py:19
  28.3 8.2 %collective-permute-start = (bf16[1,1,32,128]{3,2,1,0:T(8,128)(2,1)S(1)}, bf16[1,1,32,128]{3,2,1,0:T(8,128)(2,1)}, u32[]{:S(2)}, u32[]{:S(2)}) collective-permute-start(bf16[1,1,32,128]{3,2,1,0:T(8,128)(2,1)S(1)} %get-tuple-element.11), channel_id=1, source_target_pairs={{0,1},{1,2},{2,3},{3,4},{4,5},{5,6},{6,7},{7,8},{8,9},{9,10},{10,1... | collective-permute-start | bytes 24584 | tf_op jit(solution)/shard_map/ppermute | solution.py:17
  31.1 35.9 %copy-start.9 = (s32[1024]{0:T(1024)}, s32[1024]{0:T(1024)S(1)}, u32[]{:S(2)}) copy-start(s32[1024]{0:T(1024)S(1)} %pad_clamp_fusion) | copy-start | bytes 12292
  31.1 35.8 %copy-start.13 = (s32[16,16]{0,1:T(8,128)}, s32[16,16]{0,1:T(8,128)S(1)}, u32[]{:S(2)}) copy-start(s32[16,16]{0,1:T(8,128)S(1)} %get-tuple-element.13) | copy-start | bytes 3076
  31.1 36.6 %copy-start.14 = (f32[16,16]{0,1:T(8,128)}, f32[16,16]{0,1:T(8,128)S(1)}, u32[]{:S(2)}) copy-start(f32[16,16]{0,1:T(8,128)S(1)} %get-tuple-element.14) | copy-start | bytes 3076
  32.3 34.7 %copy-start.16 = (pred[16,16]{0,1:T(8,128)(4,1)}, pred[16,16]{0,1:T(8,128)(4,1)S(1)}, u32[]{:S(2)}) copy-start(pred[16,16]{0,1:T(8,128)(4,1)S(1)} %fusion.21) | copy-start | bytes 772
  32.3 0.6 copy-start.15
  60.4 6.6 %copy-start.2 = (bf16[96,32,128]{2,1,0:T(8,128)(2,1)S(1)}, bf16[96,32,128]{2,1,0:T(8,128)(2,1)}, u32[]{:S(2)}) copy-start(bf16[96,32,128]{2,1,0:T(8,128)(2,1)} %gather_fusion) | copy-start | bytes 2359300
  60.4 6.6 %copy-start.3 = (f32[1,16,32,128]{3,2,1,0:T(8,128)S(1)}, f32[1,16,32,128]{3,2,1,0:T(8,128)}, u32[]{:S(2)}) copy-start(f32[1,16,32,128]{3,2,1,0:T(8,128)} %param.9) | copy-start | bytes 786436
  60.4 6.6 %copy-start.4 = (f32[1,16,32,128]{3,2,1,0:T(8,128)S(1)}, f32[1,16,32,128]{3,2,1,0:T(8,128)}, u32[]{:S(2)}) copy-start(f32[1,16,32,128]{3,2,1,0:T(8,128)} %param.10) | copy-start | bytes 786436
  60.4 6.7 %copy-start.8 = (f32[1,4,32,128]{3,2,1,0:T(8,128)S(1)}, f32[1,4,32,128]{3,2,1,0:T(8,128)}, u32[]{:S(2)}) copy-start(f32[1,4,32,128]{3,2,1,0:T(8,128)} %bitcast_add_fusion.1) | copy-start | bytes 196612
  60.4 6.7 %copy-start.18 = (f32[16]{0:T(128)S(1)}, f32[16]{0:T(128)}, u32[]{:S(2)}) copy-start(f32[16]{0:T(128)} %copy-done.17) | copy-start | bytes 196
  60.4 7.4 %copy-start.10 = (f32[16,128]{1,0:T(8,128)S(1)}, f32[16,128]{1,0:T(8,128)}, u32[]{:S(2)}) copy-start(f32[16,128]{1,0:T(8,128)} %param.12) | copy-start | bytes 24580
  67.7 14.8 %copy-start.6 = (bf16[1,16,32,128]{3,2,1,0:T(8,128)(2,1)}, bf16[1,16,32,128]{3,2,1,0:T(8,128)(2,1)S(1)}, u32[]{:S(2)}) copy-start(bf16[1,16,32,128]{3,2,1,0:T(8,128)(2,1)S(1)} %get-tuple-element.5) | copy-start | bytes 393220
  68.5 14.0 %collective-permute-start.4 = (bf16[1,1,32,128]{3,2,1,0:T(8,128)(2,1)S(1)}, bf16[1,1,32,128]{3,2,1,0:T(8,128)(2,1)S(1)}, u32[]{:S(2)}, u32[]{:S(2)}) collective-permute-start(bf16[1,1,32,128]{3,2,1,0:T(8,128)(2,1)S(1)} %get-tuple-element.10), channel_id=1, source_target_pairs={{1,0},{2,1},{3,2},{4,3},{5,4},{6,5},{7,6},{8,7},{9,8},{10,9},{11,1... | collective-permute-start | bytes 24584 | tf_op jit(solution)/shard_map/ppermute | solution.py:19
  76.3 8.0 %collective-permute-start.3 = (bf16[1,1,32,128]{3,2,1,0:T(8,128)(2,1)S(1)}, bf16[1,1,32,128]{3,2,1,0:T(8,128)(2,1)S(1)}, u32[]{:S(2)}, u32[]{:S(2)}) collective-permute-start(bf16[1,1,32,128]{3,2,1,0:T(8,128)(2,1)S(1)} %get-tuple-element.9), channel_id=1, source_target_pairs={{0,1},{1,2},{2,3},{3,4},{4,5},{5,6},{6,7},{7,8},{8,9},{9,10},{10,1... | collective-permute-start | bytes 24584 | tf_op jit(solution)/shard_map/ppermute | solution.py:17
  79.2 5.0 %copy-start.7 = (f32[4,32,128]{2,1,0:T(8,128)}, f32[4,32,128]{2,1,0:T(8,128)S(1)}, u32[]{:S(2)}) copy-start(f32[4,32,128]{2,1,0:T(8,128)S(1)} %fusion.14) | copy-start | bytes 196612
  80.6 8.7 %collective-permute-start.5 = (bf16[1,4,32,128]{3,2,1,0:T(8,128)(2,1)}, bf16[1,4,32,128]{3,2,1,0:T(8,128)(2,1)}, u32[]{:S(2)}, u32[]{:S(2)}) collective-permute-start(bf16[1,4,32,128]{3,2,1,0:T(8,128)(2,1)} %fusion.19), channel_id=1, source_target_pairs={{31,0},{0,1},{1,2},{2,3},{3,4},{4,5},{5,6},{6,7},{7,8},{8,9},{9,10... | collective-permute-start | bytes 98312 | tf_op jit(solution)/shard_map/ppermute | solution.py:29
  86.9 33.6 %copy-start.12 = (f32[1,16,128]{2,1,0:T(8,128)S(1)}, f32[1,16,128]{2,1,0:T(8,128)}, u32[]{:S(2)}) copy-start(f32[1,16,128]{2,1,0:T(8,128)} %param.11) | copy-start | bytes 24580
  86.9 33.6 %copy-start.19 = (f32[16]{0:T(128)S(1)}, f32[16]{0:T(128)}, u32[]{:S(2)}) copy-start(f32[16]{0:T(128)} %copy-done.17) | copy-start | bytes 196
  114.0 6.6 %copy-start.1 = (bf16[96,32,128]{2,1,0:T(8,128)(2,1)S(1)}, bf16[96,32,128]{2,1,0:T(8,128)(2,1)}, u32[]{:S(2)}) copy-start(bf16[96,32,128]{2,1,0:T(8,128)(2,1)} %gather_fusion.1) | copy-start | bytes 2359300
  114.0 6.6 %copy-start.5 = (f32[1,16,32,128]{3,2,1,0:T(8,128)S(1)}, f32[1,16,32,128]{3,2,1,0:T(8,128)}, u32[]{:S(2)}) copy-start(f32[1,16,32,128]{3,2,1,0:T(8,128)} %param.10) | copy-start | bytes 786436
Sparse Core Ops, SparseCore 0:
  9.5 50.8 all-gather.2
  68.6 45.2 all-gather.4
where the time goes:
time: 129 us
  waiting for transfers between devices  51.7 us (40%)
  starting transfers between devices  30 us (23%)
  matrix products  17.2 us (13%)
  between operations  14.6 us (11%)
  other arithmetic  11.1 us (9%)
  local copies, waits for them, and re-layouts  4.14 us (3%)
    all_gather x2, waiting for transfers between devices, shards(): piece = lax.all_gather(weighted, 'inst', axis=0, tiled=True)  44 us
    ppermute x2, starting transfers between devices, padded(): lax.ppermute(head, axis, [((i + 1) % count, i) for i in range(count)])  19.9 us
    dot_general x2, matrix products, shards(): jnp.einsum('jt,jnrc->tnrc', coef, piece, precision=lax.Precision.HIGHEST)  13.1 us
    ppermute x2, starting transfers between devices, shifted(): return lax.ppermute(block, axis, route)  6.27 us
    ppermute x2, waiting for transfers between devices, padded(): lax.ppermute(tail, axis, [(i, (i + 1) % count) for i in range(count)])  5.31 us
    ppermute x2, starting transfers between devices, padded(): lax.ppermute(tail, axis, [(i, (i + 1) % count) for i in range(count)])  3.84 us
    gather x2, local copies, waits for them, and re-layouts, shards(): picked = lam_h[:, cols]  3.29 us
  transfers between devices with their start and end apart: 8, of which 5 were waited for; matrix products, arithmetic and copies ran while one was open for 11% of the time, Pallas kernels for 0%

commit v1 on v0

--- a/solution.py
+++ b/solution.py
@@ -69,7 +69,10 @@
             axis=1,
         )
         weighted = lam * cond_wide
-        piece = lax.all_gather(weighted, "inst", axis=0, tiled=True)
+        n_dev = lax.axis_size("inst")
+        tiles = jnp.stack([weighted for _ in range(n_dev)])
+        tiles = lax.all_to_all(tiles, "inst", split_axis=0, concat_axis=0)
+        piece = jnp.concatenate(tiles, axis=0)
         coef = lax.dynamic_slice(dspec, (0, first_inst), (piece.shape[0], local_inst))
         spec = jnp.zeros_like(weighted) + jnp.einsum(
             "jt,jnrc->tnrc", coef, piece, precision=lax.Precision.HIGHEST

time: 129 us -> 155 us (1.20)
  waiting for transfers between devices: 51.7 us -> 76.2 us
  between operations: 14.6 us -> 1.2 us
  starting transfers between devices: 30 us -> 42.2 us
  local copies, waits for them, and re-layouts: 4.14 us -> 9.87 us
  other arithmetic: 11.1 us -> 7.06 us
    all_to_all x0 -> x2, waiting for transfers between devices: none -> 67.1 us  [shards(): tiles = lax.all_to_all(tiles, 'inst', split_axis=0, concat_axis=0)]
    all_gather x2 -> x0, waiting for transfers between devices: 44 us -> none  [shards(): piece = lax.all_gather(weighted, 'inst', axis=0, tiled=True)]
    all_to_all x0 -> x2, starting transfers between devices: none -> 16.7 us  [shards(): tiles = lax.all_to_all(tiles, 'inst', split_axis=0, concat_axis=0)]
    another operation x0 -> x2, local copies, waits for them, and re-layouts: none -> 5.13 us  [shards(): tiles = jnp.stack([weighted for _ in range(n_dev)])]
    ppermute x2, starting transfers between devices: 19.9 us -> 17.6 us  [padded(): lax.ppermute(head, axis, [((i + 1) % count, i) for i in range(count)])]
    ppermute x2, starting transfers between devices: 6.27 us -> 4 us  [shifted(): return lax.ppermute(block, axis, route)]
    ppermute x2, waiting for transfers between devices: 5.31 us -> 7.18 us  [padded(): lax.ppermute(tail, axis, [(i, (i + 1) % count) for i in range(count)])]
  transfers between devices with their start and end apart: 8 -> 8, of which waited for: 5 -> 5; matrix products, arithmetic and copies ran while one was open for 11% -> 7% of each run, Pallas kernels for 0% -> 0%
where the time goes in v1:
time: 155 us; the launch traced here: 154 us
  waiting for transfers between devices  76.2 us (49%)
  starting transfers between devices  42.2 us (27%)
  matrix products  17.3 us (11%)
  local copies, waits for them, and re-layouts  9.87 us (6%)
  other arithmetic  7.06 us (5%)
    all_to_all x2, waiting for transfers between devices, shards(): tiles = lax.all_to_all(tiles, 'inst', split_axis=0, concat_axis=0)  67.1 us
    ppermute x2, starting transfers between devices, padded(): lax.ppermute(head, axis, [((i + 1) % count, i) for i in range(count)])  17.6 us
    all_to_all x2, starting transfers between devices, shards(): tiles = lax.all_to_all(tiles, 'inst', split_axis=0, concat_axis=0)  16.7 us
    dot_general x2, matrix products, shards(): jnp.einsum('jt,jnrc->tnrc', coef, piece, precision=lax.Precision.HIGHEST)  13.1 us
    ppermute x2, waiting for transfers between devices, padded(): lax.ppermute(tail, axis, [(i, (i + 1) % count) for i in range(count)])  7.18 us
    another operation x2, local copies, waits for them, and re-layouts, shards(): tiles = jnp.stack([weighted for _ in range(n_dev)])  5.13 us
    ppermute x2, starting transfers between devices, shifted(): return lax.ppermute(block, axis, route)  4 us
    ppermute x2, starting transfers between devices, padded(): lax.ppermute(tail, axis, [(i, (i + 1) % count) for i in range(count)])  3.84 us
  transfers between devices with their start and end apart: 8, of which 5 were waited for; matrix products, arithmetic and copies ran while one was open for 7% of the time, Pallas kernels for 0%

profile of v1, /device:TPU:1, one launch (start us, length us, event | category | flops | bytes accessed | tf_op | source)
XLA Modules:
  0.0 153.8 jit_solution(2594864123116944374)
XLA Ops:
  0.0 0.0 copy-start
  0.8 0.0 copy-start.16
  0.8 0.5 copy-done.16
  1.3 1.1 multiply_convert_fusion
  2.4 2.6 %stack.4 = f32[16,1,16,32,128]{4,3,2,1,0:T(8,128)} broadcast(f32[16,32,128]{2,1,0:T(8,128)S(1)} %get-tuple-element.8), dimensions={2,3,4} | broadcast | bytes 4456448 | tf_op jit(solution)/shard_map/stack | solution.py:73
  5.0 11.3 %all-to-all-start = ((f32[16,1,16,32,128]{4,3,2,1,0:T(8,128)}), f32[16,1,16,32,128]{4,3,2,1,0:T(8,128)}, u32[]{:S(2)}, u32[]{:S(2)}) async-start(f32[16,1,16,32,128]{4,3,2,1,0:T(8,128)} %stack.4), calls=%async_computation | async-start | bytes 8388608 | tf_op jit(solution)/shard_map/all_to_all | solution.py:74
  16.2 0.0 copy-done.21
  16.2 0.0 copy-start.10
  16.3 0.0 copy-start.19
  16.3 0.0 copy-done.6
  16.3 0.1 fusion.16
  16.4 0.7 fusion.18
  17.1 1.9 %collective-permute-start.2 = (bf16[1,4,32,128]{3,2,1,0:T(8,128)(2,1)}, bf16[1,4,32,128]{3,2,1,0:T(8,128)(2,1)S(1)}, u32[]{:S(2)}, u32[]{:S(2)}) collective-permute-start(bf16[1,4,32,128]{3,2,1,0:T(8,128)(2,1)} %fusion.18), channel_id=1, source_target_pairs={{31,0},{0,1},{1,2},{2,3},{3,4},{4,5},{5,6},{6,7},{7,8},{8,9},{9,10... | collective-permute-start | bytes 98312 | tf_op jit(solution)/shard_map/ppermute | solution.py:29
  19.1 9.1 %collective-permute-start.1 = (bf16[1,1,32,128]{3,2,1,0:T(8,128)(2,1)S(1)}, bf16[1,1,32,128]{3,2,1,0:T(8,128)(2,1)S(1)}, u32[]{:S(2)}, u32[]{:S(2)}) collective-permute-start(bf16[1,1,32,128]{3,2,1,0:T(8,128)(2,1)S(1)} %get-tuple-element.12), channel_id=1, source_target_pairs={{1,0},{2,1},{3,2},{4,3},{5,4},{6,5},{7,6},{8,7},{9,8},{10,9},{11,1... | collective-permute-start | bytes 24584 | tf_op jit(solution)/shard_map/ppermute | solution.py:19
  28.2 1.9 %collective-permute-start = (bf16[1,1,32,128]{3,2,1,0:T(8,128)(2,1)S(1)}, bf16[1,1,32,128]{3,2,1,0:T(8,128)(2,1)}, u32[]{:S(2)}, u32[]{:S(2)}) collective-permute-start(bf16[1,1,32,128]{3,2,1,0:T(8,128)(2,1)S(1)} %get-tuple-element.11), channel_id=1, source_target_pairs={{0,1},{1,2},{2,3},{3,4},{4,5},{5,6},{6,7},{7,8},{8,9},{9,10},{10,1... | collective-permute-start | bytes 24584 | tf_op jit(solution)/shard_map/ppermute | solution.py:17
  30.1 0.0 copy-done.19
  30.2 0.0 copy-done.18
  30.2 0.1 copy.11
  30.3 0.1 reshape.89
  30.4 0.0 copy-start.8
  30.4 0.0 copy-start.12
  30.4 0.0 copy-start.13
  30.4 0.6 broadcast_subtract_fusion
  31.0 0.0 collective-permute-done.1
  31.0 0.0 copy-start.14
  31.0 0.6 copy-done.14
  31.6 4.9 %collective-permute-done = bf16[1,1,32,128]{3,2,1,0:T(8,128)(2,1)} collective-permute-done((bf16[1,1,32,128]{3,2,1,0:T(8,128)(2,1)S(1)}, bf16[1,1,32,128]{3,2,1,0:T(8,128)(2,1)}, u32[]{:S(2)}, u32[]{:S(2)}) %collective-permute-start) | collective-permute-done | bytes 8224 | tf_op jit(solution)/shard_map/ppermute | solution.py:17
  36.5 0.7 maximum_bitcast_fusion
  37.2 1.6 %gather_fusion = bf16[96,32,128]{2,1,0:T(8,128)(2,1)} fusion(bf16[18,32,128]{2,1,0:T(8,128)(2,1)S(1)} %maximum_bitcast_fusion, s32[1024]{0:T(1024)S(1)} %pad_clamp_fusion), kind=kCustom, calls=%fused_computation | custom fusion | bytes 1573248 | tf_op jit(solution)/shard_map/gather | solution.py:57
  38.9 0.0 collective-permute-done.2
  38.9 1.4 bitcast_add_fusion.1
  40.3 32.6 %all-to-all-done = f32[16,1,16,32,128]{4,3,2,1,0:T(8,128)} async-done(((f32[16,1,16,32,128]{4,3,2,1,0:T(8,128)}), f32[16,1,16,32,128]{4,3,2,1,0:T(8,128)}, u32[]{:S(2)}, u32[]{:S(2)}) %all-to-all-start) | async-done | bytes 4194336 | tf_op jit(solution)/shard_map/all_to_all | solution.py:74
  72.8 6.5 %fusion.2 = f32[1,16,32,128]{3,0,2,1:T(1,128)S(1)} fusion(f32[16,16,32,128]{3,2,1,0:T(8,128)} %bitcast.17, f32[16,16]{0,1:T(8,128)S(1)} %get-tuple-element.14, s32[]{:T(128)S(6)} %select_n.31, pred[16,16]{0,1:T(8,128)(4,1)S(1)} %fusion.21, s32[16,16]{0,1:T(8,128)S(1)} %get-tuple-element.13), kind=kOutput, calls=%fused_computation.4 | convolution fusion | flops 12583056 | bytes 4457988 | tf_op jit(solution)/shard_map/jt,jnrc->tnrc/dot_general | solution.py:77
  79.3 0.0 copy-done.8
  79.4 0.0 copy-done.12
  79.4 0.0 copy-done.15
  79.4 0.0 copy-done
  79.4 0.0 copy-done.10
  79.4 0.0 copy-done.2
  79.4 0.0 copy-done.7
  79.4 1.7 %fusion.32 = (bf16[1,16,32,128]{3,2,1,0:T(8,128)(2,1)S(1)}, f32[1,16,32,128]{3,2,1,0:T(8,128)S(1)}) fusion(f32[1,16,32,128]{3,2,1,0:T(8,128)} %param.10, f32[1,16,32,128]{3,2,1,0:T(8,128)S(1)} %bitcast.81, f32[1,4,32,128]{3,2,1,0:T(8,128)S(1)} %copy-done.7, f32[16,128]{1,0:T(8,128)S(1)} %bitcast.82, f32[1,16,32,128]{3,2,1,0:T(8,128)} %param.9, ...), kind=kOutput, calls=%fused_computation.55 | convolution fusion | flops 101187584 | bytes 5185600 | tf_op jit(solution)/shard_map/tnkri,tnkio->tnro/dot_general | solution.py:58
  81.1 0.0 copy-done.13
  81.1 0.0 copy-start.4
  81.2 0.0 copy-done.9
  81.2 2.6 %stack.5 = f32[16,1,16,32,128]{4,3,2,1,0:T(8,128)} broadcast(f32[16,32,128]{2,1,0:T(8,128)S(1)} %multiply_bitcast_fusion), dimensions={2,3,4} | broadcast | bytes 4456448 | tf_op jit(solution)/shard_map/stack | solution.py:73
  83.8 5.5 %all-to-all-start.1 = ((f32[16,1,16,32,128]{4,3,2,1,0:T(8,128)}), f32[16,1,16,32,128]{4,3,2,1,0:T(8,128)}, u32[]{:S(2)}, u32[]{:S(2)}) async-start(f32[16,1,16,32,128]{4,3,2,1,0:T(8,128)} %stack.5), calls=%async_computation.1 | async-start | bytes 8388608 | tf_op jit(solution)/shard_map/all_to_all | solution.py:74
  89.2 8.4 %collective-permute-start.4 = (bf16[1,1,32,128]{3,2,1,0:T(8,128)(2,1)S(1)}, bf16[1,1,32,128]{3,2,1,0:T(8,128)(2,1)S(1)}, u32[]{:S(2)}, u32[]{:S(2)}) collective-permute-start(bf16[1,1,32,128]{3,2,1,0:T(8,128)(2,1)S(1)} %get-tuple-element.10), channel_id=1, source_target_pairs={{1,0},{2,1},{3,2},{4,3},{5,4},{6,5},{7,6},{8,7},{9,8},{10,9},{11,1... | collective-permute-start | bytes 24584 | tf_op jit(solution)/shard_map/ppermute | solution.py:19
  97.7 1.9 %collective-permute-start.3 = (bf16[1,1,32,128]{3,2,1,0:T(8,128)(2,1)S(1)}, bf16[1,1,32,128]{3,2,1,0:T(8,128)(2,1)S(1)}, u32[]{:S(2)}, u32[]{:S(2)}) collective-permute-start(bf16[1,1,32,128]{3,2,1,0:T(8,128)(2,1)S(1)} %get-tuple-element.9), channel_id=1, source_target_pairs={{0,1},{1,2},{2,3},{3,4},{4,5},{5,6},{6,7},{7,8},{8,9},{9,10},{10,1... | collective-permute-start | bytes 24584 | tf_op jit(solution)/shard_map/ppermute | solution.py:17
  99.6 1.1 fusion.14
  100.7 0.7 fusion.19
  101.4 2.1 %collective-permute-start.5 = (bf16[1,4,32,128]{3,2,1,0:T(8,128)(2,1)}, bf16[1,4,32,128]{3,2,1,0:T(8,128)(2,1)}, u32[]{:S(2)}, u32[]{:S(2)}) collective-permute-start(bf16[1,4,32,128]{3,2,1,0:T(8,128)(2,1)} %fusion.19), channel_id=1, source_target_pairs={{31,0},{0,1},{1,2},{2,3},{3,4},{4,5},{5,6},{6,7},{7,8},{8,9},{9,10... | collective-permute-start | bytes 98312 | tf_op jit(solution)/shard_map/ppermute | solution.py:29
  103.5 0.0 collective-permute-done.4
  103.5 2.3 %collective-permute-done.3 = bf16[1,1,32,128]{3,2,1,0:T(8,128)(2,1)S(1)} collective-permute-done((bf16[1,1,32,128]{3,2,1,0:T(8,128)(2,1)S(1)}, bf16[1,1,32,128]{3,2,1,0:T(8,128)(2,1)S(1)}, u32[]{:S(2)}, u32[]{:S(2)}) %collective-permute-start.3) | collective-permute-done | bytes 8224 | tf_op jit(solution)/shard_map/ppermute | solution.py:17
  105.8 0.9 maximum_bitcast_fusion.1
  106.7 1.8 %gather_fusion.1 = bf16[96,32,128]{2,1,0:T(8,128)(2,1)} fusion(bf16[18,32,128]{2,1,0:T(8,128)(2,1)S(1)} %maximum_bitcast_fusion.1, s32[1024]{0:T(1024)} %copy-done.8), kind=kCustom, calls=%fused_computation.1 | custom fusion | bytes 1573248 | tf_op jit(solution)/shard_map/gather | solution.py:57
  108.5 1.9 %collective-permute-done.5 = bf16[1,4,32,128]{3,2,1,0:T(8,128)(2,1)} collective-permute-done((bf16[1,4,32,128]{3,2,1,0:T(8,128)(2,1)}, bf16[1,4,32,128]{3,2,1,0:T(8,128)(2,1)}, u32[]{:S(2)}, u32[]{:S(2)}) %collective-permute-start.5) | collective-permute-done | bytes 32800 | tf_op jit(solution)/shard_map/ppermute | solution.py:29
  110.4 0.9 bitcast_add_fusion
  111.3 34.5 %all-to-all-done.1 = f32[16,1,16,32,128]{4,3,2,1,0:T(8,128)} async-done(((f32[16,1,16,32,128]{4,3,2,1,0:T(8,128)}), f32[16,1,16,32,128]{4,3,2,1,0:T(8,128)}, u32[]{:S(2)}, u32[]{:S(2)}) %all-to-all-start.1) | async-done | bytes 4194336 | tf_op jit(solution)/shard_map/all_to_all | solution.py:74
  145.8 6.5 %fusion = f32[1,16,32,128]{3,0,2,1:T(1,128)S(1)} fusion(f32[16,16,32,128]{3,2,1,0:T(8,128)} %bitcast.32, f32[16,16]{0,1:T(8,128)} %copy-done.13, s32[]{:T(128)S(6)} %select_n.31, pred[16,16]{0,1:T(8,128)(4,1)} %copy-done.15, s32[16,16]{0,1:T(8,128)} %copy-done.12), kind=kOutput, calls=%fused_computation.2 | convolution fusion | flops 12583056 | bytes 4457988 | tf_op jit(solution)/shard_map/jt,jnrc->tnrc/dot_general | solution.py:77
  152.4 0.0 copy-done.11
  152.4 0.0 copy-done.17
  152.4 0.0 copy-done.1
  152.4 0.0 copy-done.3
  152.4 1.4 multiply_add_fusion
  (25 shorter events, 0.1 us)
Async XLA Ops:
  0.0 79.4 %copy-start = (bf16[1,16,6,128,128]{4,3,2,1,0:T(8,128)(2,1)S(1)}, bf16[1,16,6,128,128]{4,3,2,1,0:T(8,128)(2,1)}, u32[]{:S(2)}) copy-start(bf16[1,16,6,128,128]{4,3,2,1,0:T(8,128)(2,1)} %param.13) | copy-start | bytes 9437188
  0.8 0.5 copy-start.16
  5.0 11.3 %copy-start.21 = (s32[1,4]{1,0:T(1,128)S(1)}, s32[1,4]{1,0:T(1,128)}, u32[]{:S(2)}) copy-start(s32[1,4]{1,0:T(1,128)} %param.16) | copy-start | bytes 52
  5.0 11.3 %copy-start.6 = (bf16[1,4,128,128]{3,2,1,0:T(8,128)(2,1)S(1)}, bf16[1,4,128,128]{3,2,1,0:T(8,128)(2,1)}, u32[]{:S(2)}) copy-start(bf16[1,4,128,128]{3,2,1,0:T(8,128)(2,1)} %param.14) | copy-start | bytes 393220
  5.0 25.2 %copy-start.18 = (s32[16,6]{0,1:T(8,128)S(1)}, s32[16,6]{0,1:T(8,128)}, u32[]{:S(2)}) copy-start(s32[16,6]{0,1:T(8,128)} %param.15) | copy-start | bytes 1156
  5.0 67.9 %all-to-all-start = ((f32[16,1,16,32,128]{4,3,2,1,0:T(8,128)}), f32[16,1,16,32,128]{4,3,2,1,0:T(8,128)}, u32[]{:S(2)}, u32[]{:S(2)}) async-start(f32[16,1,16,32,128]{4,3,2,1,0:T(8,128)} %stack.4), calls=%async_computation | async-start | bytes 8388608 | tf_op jit(solution)/shard_map/all_to_all | solution.py:74
  16.2 63.2 %copy-start.10 = (f32[1,16,128]{2,1,0:T(8,128)S(1)}, f32[1,16,128]{2,1,0:T(8,128)}, u32[]{:S(2)}) copy-start(f32[1,16,128]{2,1,0:T(8,128)} %param.11) | copy-start | bytes 24580
  16.3 13.9 %copy-start.19 = (f32[4]{0:T(128)}, f32[4]{0:T(128)S(1)}, u32[]{:S(2)}) copy-start(f32[4]{0:T(128)S(1)} %convert_bitcast_fusion) | copy-start | bytes 52
  17.1 21.8 %collective-permute-start.2 = (bf16[1,4,32,128]{3,2,1,0:T(8,128)(2,1)}, bf16[1,4,32,128]{3,2,1,0:T(8,128)(2,1)S(1)}, u32[]{:S(2)}, u32[]{:S(2)}) collective-permute-start(bf16[1,4,32,128]{3,2,1,0:T(8,128)(2,1)} %fusion.18), channel_id=1, source_target_pairs={{31,0},{0,1},{1,2},{2,3},{3,4},{4,5},{5,6},{6,7},{7,8},{8,9},{9,10... | collective-permute-start | bytes 98312 | tf_op jit(solution)/shard_map/ppermute | solution.py:29
  19.1 12.0 %collective-permute-start.1 = (bf16[1,1,32,128]{3,2,1,0:T(8,128)(2,1)S(1)}, bf16[1,1,32,128]{3,2,1,0:T(8,128)(2,1)S(1)}, u32[]{:S(2)}, u32[]{:S(2)}) collective-permute-start(bf16[1,1,32,128]{3,2,1,0:T(8,128)(2,1)S(1)} %get-tuple-element.12), channel_id=1, source_target_pairs={{1,0},{2,1},{3,2},{4,3},{5,4},{6,5},{7,6},{8,7},{9,8},{10,9},{11,1... | collective-permute-start | bytes 24584 | tf_op jit(solution)/shard_map/ppermute | solution.py:19
  28.2 8.3 %collective-permute-start = (bf16[1,1,32,128]{3,2,1,0:T(8,128)(2,1)S(1)}, bf16[1,1,32,128]{3,2,1,0:T(8,128)(2,1)}, u32[]{:S(2)}, u32[]{:S(2)}) collective-permute-start(bf16[1,1,32,128]{3,2,1,0:T(8,128)(2,1)S(1)} %get-tuple-element.11), channel_id=1, source_target_pairs={{0,1},{1,2},{2,3},{3,4},{4,5},{5,6},{6,7},{7,8},{8,9},{9,10},{10,1... | collective-permute-start | bytes 24584 | tf_op jit(solution)/shard_map/ppermute | solution.py:17
  30.4 49.0 %copy-start.8 = (s32[1024]{0:T(1024)}, s32[1024]{0:T(1024)S(1)}, u32[]{:S(2)}) copy-start(s32[1024]{0:T(1024)S(1)} %pad_clamp_fusion) | copy-start | bytes 12292
  30.4 49.0 %copy-start.12 = (s32[16,16]{0,1:T(8,128)}, s32[16,16]{0,1:T(8,128)S(1)}, u32[]{:S(2)}) copy-start(s32[16,16]{0,1:T(8,128)S(1)} %get-tuple-element.13) | copy-start | bytes 3076
  30.4 50.7 %copy-start.13 = (f32[16,16]{0,1:T(8,128)}, f32[16,16]{0,1:T(8,128)S(1)}, u32[]{:S(2)}) copy-start(f32[16,16]{0,1:T(8,128)S(1)} %get-tuple-element.14) | copy-start | bytes 3076
  31.0 48.4 %copy-start.15 = (pred[16,16]{0,1:T(8,128)(4,1)}, pred[16,16]{0,1:T(8,128)(4,1)S(1)}, u32[]{:S(2)}) copy-start(pred[16,16]{0,1:T(8,128)(4,1)S(1)} %fusion.21) | copy-start | bytes 772
  31.0 0.6 copy-start.14
  72.8 6.6 %copy-start.2 = (bf16[96,32,128]{2,1,0:T(8,128)(2,1)S(1)}, bf16[96,32,128]{2,1,0:T(8,128)(2,1)}, u32[]{:S(2)}) copy-start(bf16[96,32,128]{2,1,0:T(8,128)(2,1)} %gather_fusion) | copy-start | bytes 2359300
  72.8 6.6 %copy-start.7 = (f32[1,4,32,128]{3,2,1,0:T(8,128)S(1)}, f32[1,4,32,128]{3,2,1,0:T(8,128)}, u32[]{:S(2)}) copy-start(f32[1,4,32,128]{3,2,1,0:T(8,128)} %bitcast_add_fusion.1) | copy-start | bytes 196612
  72.8 8.3 %copy-start.9 = (f32[16,128]{1,0:T(8,128)S(1)}, f32[16,128]{1,0:T(8,128)}, u32[]{:S(2)}) copy-start(f32[16,128]{1,0:T(8,128)} %param.12) | copy-start | bytes 24580
  81.1 18.5 %copy-start.4 = (bf16[1,16,32,128]{3,2,1,0:T(8,128)(2,1)}, bf16[1,16,32,128]{3,2,1,0:T(8,128)(2,1)S(1)}, u32[]{:S(2)}) copy-start(bf16[1,16,32,128]{3,2,1,0:T(8,128)(2,1)S(1)} %get-tuple-element.5) | copy-start | bytes 393220
  83.8 16.9 %copy-start.20 = (f32[4]{0:T(128)S(1)}, f32[4]{0:T(128)}, u32[]{:S(2)}) copy-start(f32[4]{0:T(128)} %copy-done.19) | copy-start | bytes 52
  83.8 62.1 %all-to-all-start.1 = ((f32[16,1,16,32,128]{4,3,2,1,0:T(8,128)}), f32[16,1,16,32,128]{4,3,2,1,0:T(8,128)}, u32[]{:S(2)}, u32[]{:S(2)}) async-start(f32[16,1,16,32,128]{4,3,2,1,0:T(8,128)} %stack.5), calls=%async_computation.1 | async-start | bytes 8388608 | tf_op jit(solution)/shard_map/all_to_all | solution.py:74
  89.2 14.2 %collective-permute-start.4 = (bf16[1,1,32,128]{3,2,1,0:T(8,128)(2,1)S(1)}, bf16[1,1,32,128]{3,2,1,0:T(8,128)(2,1)S(1)}, u32[]{:S(2)}, u32[]{:S(2)}) collective-permute-start(bf16[1,1,32,128]{3,2,1,0:T(8,128)(2,1)S(1)} %get-tuple-element.10), channel_id=1, source_target_pairs={{1,0},{2,1},{3,2},{4,3},{5,4},{6,5},{7,6},{8,7},{9,8},{10,9},{11,1... | collective-permute-start | bytes 24584 | tf_op jit(solution)/shard_map/ppermute | solution.py:19
  97.7 8.1 %collective-permute-start.3 = (bf16[1,1,32,128]{3,2,1,0:T(8,128)(2,1)S(1)}, bf16[1,1,32,128]{3,2,1,0:T(8,128)(2,1)S(1)}, u32[]{:S(2)}, u32[]{:S(2)}) collective-permute-start(bf16[1,1,32,128]{3,2,1,0:T(8,128)(2,1)S(1)} %get-tuple-element.9), channel_id=1, source_target_pairs={{0,1},{1,2},{2,3},{3,4},{4,5},{5,6},{6,7},{7,8},{8,9},{9,10},{10,1... | collective-permute-start | bytes 24584 | tf_op jit(solution)/shard_map/ppermute | solution.py:17
  100.7 2.8 %copy-start.5 = (f32[4,32,128]{2,1,0:T(8,128)}, f32[4,32,128]{2,1,0:T(8,128)S(1)}, u32[]{:S(2)}) copy-start(f32[4,32,128]{2,1,0:T(8,128)S(1)} %fusion.14) | copy-start | bytes 196612
  101.4 9.0 %collective-permute-start.5 = (bf16[1,4,32,128]{3,2,1,0:T(8,128)(2,1)}, bf16[1,4,32,128]{3,2,1,0:T(8,128)(2,1)}, u32[]{:S(2)}, u32[]{:S(2)}) collective-permute-start(bf16[1,4,32,128]{3,2,1,0:T(8,128)(2,1)} %fusion.19), channel_id=1, source_target_pairs={{31,0},{0,1},{1,2},{2,3},{3,4},{4,5},{5,6},{6,7},{7,8},{8,9},{9,10... | collective-permute-start | bytes 98312 | tf_op jit(solution)/shard_map/ppermute | solution.py:29
  108.5 43.9 %copy-start.11 = (f32[1,16,128]{2,1,0:T(8,128)S(1)}, f32[1,16,128]{2,1,0:T(8,128)}, u32[]{:S(2)}) copy-start(f32[1,16,128]{2,1,0:T(8,128)} %param.11) | copy-start | bytes 24580
  108.5 43.9 %copy-start.17 = (f32[16]{0:T(128)S(1)}, f32[16]{0:T(128)}, u32[]{:S(2)}) copy-start(f32[16]{0:T(128)} %copy-done.16) | copy-start | bytes 196
  145.8 6.6 %copy-start.1 = (bf16[96,32,128]{2,1,0:T(8,128)(2,1)S(1)}, bf16[96,32,128]{2,1,0:T(8,128)(2,1)}, u32[]{:S(2)}) copy-start(bf16[96,32,128]{2,1,0:T(8,128)(2,1)} %gather_fusion.1) | copy-start | bytes 2359300
  145.8 6.6 %copy-start.3 = (f32[1,16,32,128]{3,2,1,0:T(8,128)S(1)}, f32[1,16,32,128]{3,2,1,0:T(8,128)}, u32[]{:S(2)}) copy-start(f32[1,16,32,128]{3,2,1,0:T(8,128)} %param.10) | copy-start | bytes 786436
